TPU v7x, 32 devices: a whole 2x2x4 slice. The times are simulated.
32 devices in a mesh: dp: 8 (over z, core), mp: 4 (over y, x).
Axes of the slice: x: 2, y: 2, z: 4, core: 2. Of those that a mesh axis runs over, the one named last changes fastest.
Arguments:
- tokens: bfloat16 [65536, 1024], P('dp'), may hold values from -7 to 7
- segments: int32 [64, 1024], P('dp'), may hold values from 0 to 3, never falling along the last dimension, each value on 1 to 512 neighbouring positions
- routes: int32 [64, 128], P('dp'), may hold values from 0 to 1023, as said below
- cotangent: bfloat16 [65536, 1024], P('dp'), may hold values from -6 to 6
- gain_attn: bfloat16 [1024], replicated, may hold values from 0.5 to 1.5
- gain_mlp: bfloat16 [1024], replicated, may hold values from 0.5 to 1.5
- w_router: bfloat16 [1024], replicated, may hold values from -1 to 1
- w_qkv: bfloat16 [1024, 3072], P(None, 'mp'), may hold values from -0.1875 to 0.1875
- w_out: bfloat16 [1024, 1024], P('mp'), may hold values from -0.75 to 0.75
- w_up: bfloat16 [1024, 4096], P(None, 'mp'), may hold values from -0.1875 to 0.1875
- w_down: bfloat16 [4096, 1024], P('mp'), may hold values from -0.09375 to 0.09375
Outputs:
- output: bfloat16 [65536, 1024], P('dp')
- grad_tokens: bfloat16 [65536, 1024], P('dp')
- grad_gain_attn: float32 [1024], replicated
- grad_gain_mlp: float32 [1024], replicated
- grad_router: float32 [1024], replicated
- grad_qkv: float32 [1024, 3072], P(None, 'mp')
- grad_out: float32 [1024, 1024], P('mp')
- grad_up: float32 [1024, 4096], P(None, 'mp')
- grad_down: float32 [4096, 1024], P('mp')
- routed_share: float32 [], replicated
- mean_score: float32 [], replicated
Inputs may be any that keep to these rules, and one draw needn't show every extreme that they name: `routes`: each row holds 128 different positions of its sequence in ascending order, the first 0 and the last 1023. The segment numbers of one sequence never fall; each of the 4 segments has 1 to 512 positions, one exactly 512.
All inputs are finite; a program needn't handle non-finite values.
Results may differ from a plain program's by a relative error of at most 0.012.
Values may be sent and summed in bfloat16 or wider, within the bound.
No kernel may reach another device: no remote copies, remote signals or barrier semaphores. Data moves between devices by JAX's collectives and lax.ppermute only.
A program may use at most 256 MiB of HBM per device.

v0:
```python
import jax
import jax.numpy as jnp
from jax import lax
from jax.sharding import PartitionSpec as P

HD = 64


def rms_scale(inputs, gain_vec):
    inverse = lax.rsqrt(jnp.mean(inputs * inputs, axis=-1, keepdims=True) + 1e-06)
    return inputs * inverse * gain_vec


def transposed(left, right):
    return lax.dot_general(
        left, right, (((0,), (0,)), ((), ())), preferred_element_type=jnp.float32
    )


def shards(
    tokens, segments, routes, cotangent, gain_attn, gain_mlp, w_router, w_qkv, w_out, w_up, w_down
):
    seq_count, seq_len = segments.shape
    routed = routes.shape[1]
    local_heads = w_out.shape[0] // HD
    scale = HD ** (-0.5)
    row_total = seq_count * routed
    offsets = lax.broadcasted_iota(jnp.int32, (seq_count, routed), 0) * seq_len
    picks = (routes + offsets).reshape(-1)
    logits = jnp.dot(tokens, w_router, preferred_element_type=jnp.float32)
    scores = jax.nn.sigmoid(logits)
    rate_routed = scores[picks]
    routed_local = jnp.sum(rate_routed)
    score_local = jnp.sum(scores)
    routed_total, score_total = lax.psum((routed_local, score_local), "dp")
    rows_routed = tokens[picks].astype(jnp.float32)
    grad_rows = cotangent[picks].astype(jnp.float32)
    seg_routed = segments.reshape(-1)[picks].reshape(seq_count, routed)
    gain_one = gain_attn.astype(jnp.float32)
    gain_two = gain_mlp.astype(jnp.float32)
    router_vec = w_router.astype(jnp.float32)
    normed_one = rms_scale(rows_routed, gain_one).astype(jnp.bfloat16)
    joint_qkv = jnp.dot(normed_one, w_qkv, preferred_element_type=jnp.float32).astype(jnp.bfloat16)
    joint_qkv = joint_qkv.reshape(seq_count, routed, local_heads, 3, HD)
    queries = joint_qkv[:, :, :, 0]
    key_rows = joint_qkv[:, :, :, 1]
    values = joint_qkv[:, :, :, 2]
    causal = lax.broadcasted_iota(jnp.int32, (routed, routed), 0) >= lax.broadcasted_iota(
        jnp.int32, (routed, routed), 1
    )
    allowed = causal[None, None] & (seg_routed[:, None, :, None] == seg_routed[:, None, None, :])

    def masked_scores():
        raw_scores = (
            jnp.einsum("sqhe,skhe->shqk", queries, key_rows, preferred_element_type=jnp.float32)
            * scale
        )
        return jnp.where(allowed, raw_scores, -1e30)

    masked = masked_scores()
    top_score = jnp.max(masked, axis=-1, keepdims=True)
    expon_terms = jnp.exp(masked - top_score)
    totals = jnp.sum(expon_terms, axis=-1, keepdims=True)
    probs = expon_terms / totals
    log_total = top_score + jnp.log(totals)
    mixed = jnp.einsum(
        "shqk,skhe->sqhe", probs.astype(jnp.bfloat16), values, preferred_element_type=jnp.float32
    )
    heads_out = mixed.astype(jnp.bfloat16).reshape(row_total, local_heads * HD)
    rate_col = rate_routed[:, None]
    attended = lax.psum(jnp.dot(heads_out, w_out, preferred_element_type=jnp.float32), "mp")
    middle = rows_routed + attended
    normed_two = rms_scale(middle, gain_two).astype(jnp.bfloat16)
    pre_act = jnp.dot(normed_two, w_up, preferred_element_type=jnp.float32)
    hidden = jax.nn.gelu(pre_act).astype(jnp.bfloat16)
    mlp_out = lax.psum(jnp.dot(hidden, w_down, preferred_element_type=jnp.float32), "mp")
    delta_rows = attended + mlp_out
    updated_low = (rows_routed + rate_col * delta_rows).astype(jnp.bfloat16)
    router_term = jnp.sum(grad_rows * delta_rows, axis=-1) * rate_routed * (1.0 - rate_routed)
    output = tokens.at[picks].set(updated_low)
    grad_mlp_out = (rate_col * grad_rows).astype(jnp.bfloat16)
    grad_down = transposed(hidden, grad_mlp_out)
    grad_hidden = jnp.dot(grad_mlp_out, w_down.T, preferred_element_type=jnp.float32)
    unused, gelu_pull = jax.vjp(jax.nn.gelu, pre_act)
    grad_pre = gelu_pull(grad_hidden)[0].astype(jnp.bfloat16)
    grad_up = transposed(normed_two, grad_pre)
    grad_normed_two = lax.psum(jnp.dot(grad_pre, w_up.T, preferred_element_type=jnp.float32), "mp")
    unused, second_pull = jax.vjp(rms_scale, middle, gain_two)
    grad_middle, grad_gain_mlp = second_pull(grad_normed_two)
    grad_attended = (rate_col * grad_rows + grad_middle).astype(jnp.bfloat16)
    grad_out = transposed(heads_out, grad_attended)
    grad_mixed = jnp.dot(grad_attended, w_out.T, preferred_element_type=jnp.float32).astype(
        jnp.bfloat16
    )
    grad_mixed = grad_mixed.reshape(seq_count, routed, local_heads, HD)
    again = masked_scores()
    probs_again = jnp.exp(again - log_total)
    probs_low = probs_again.astype(jnp.bfloat16)
    grad_values = jnp.einsum(
        "shqk,sqhe->skhe", probs_low, grad_mixed, preferred_element_type=jnp.float32
    )
    grad_probs = jnp.einsum(
        "sqhe,skhe->shqk", grad_mixed, values, preferred_element_type=jnp.float32
    )
    row_dots = jnp.sum(probs_again * grad_probs, axis=-1, keepdims=True)
    grad_logits = (probs_again * (grad_probs - row_dots)).astype(jnp.bfloat16)
    grad_queries = (
        jnp.einsum("shqk,skhe->sqhe", grad_logits, key_rows, preferred_element_type=jnp.float32)
        * scale
    )
    grad_keys = (
        jnp.einsum("shqk,sqhe->skhe", grad_logits, queries, preferred_element_type=jnp.float32)
        * scale
    )
    grad_joint = jnp.stack([grad_queries, grad_keys, grad_values], axis=3).astype(jnp.bfloat16)
    grad_joint = grad_joint.reshape(row_total, local_heads * 3 * HD)
    grad_qkv = transposed(normed_one, grad_joint)
    grad_normed_one = lax.psum(
        jnp.dot(grad_joint, w_qkv.T, preferred_element_type=jnp.float32), "mp"
    )
    unused, first_pull = jax.vjp(rms_scale, rows_routed, gain_one)
    grad_first, grad_gain_attn = first_pull(grad_normed_one)
    grad_router = jnp.sum(router_term[:, None] * rows_routed, axis=0)
    grad_routed_rows = (
        grad_rows + grad_middle + grad_first + router_term[:, None] * router_vec[None, :]
    )
    grad_rows_low = grad_routed_rows.astype(jnp.bfloat16)
    grad_tokens = cotangent.at[picks].set(grad_rows_low)
    grad_gain_attn, grad_gain_mlp, grad_router, grad_qkv, grad_out, grad_up, grad_down = lax.psum(
        (grad_gain_attn, grad_gain_mlp, grad_router, grad_qkv, grad_out, grad_up, grad_down), "dp"
    )
    token_count = seq_count * seq_len * lax.axis_size("dp")
    routed_share = routed_total / score_total
    mean_score = score_total / token_count
    return (
        output,
        grad_tokens,
        grad_gain_attn,
        grad_gain_mlp,
        grad_router,
        grad_qkv,
        grad_out,
        grad_up,
        grad_down,
        routed_share,
        mean_score,
    )


def solution(mesh):
    in_specs = (
        P("dp", None),
        P("dp", None),
        P("dp", None),
        P("dp", None),
        P(),
        P(),
        P(),
        P(None, "mp"),
        P("mp", None),
        P(None, "mp"),
        P("mp", None),
    )
    out_specs = (
        P("dp", None),
        P("dp", None),
        P(),
        P(),
        P(),
        P(None, "mp"),
        P("mp", None),
        P(None, "mp"),
        P("mp", None),
        P(),
        P(),
    )
    return jax.shard_map(shards, mesh=mesh, in_specs=in_specs, out_specs=out_specs, check_vma=False)
```

profile of v0, /device:TPU:0, one launch (start us, length us, event | category | flops | bytes accessed | tf_op | source)
XLA Modules:
  0.0 775.4 jit_solution(11880056417674116861)
XLA Ops:
  7.3 14.9 %copy.102 = bf16[8192,1024]{1,0:T(8,128)(2,1)} copy(bf16[8192,1024]{1,0:T(8,128)(2,1)} %param.11) | data formatting | bytes 33554432
  22.2 2.1 copy-done.11
  24.3 6.2 copy.103
  30.5 13.9 %gather_fusion = bf16[1024,1024]{1,0:T(8,128)(2,1)} fusion(bf16[8192,1024]{1,0:T(8,128)(2,1)} %copy.102, s32[1024]{0:T(1024)S(1)} %broadcast_clamp_fusion), kind=kCustom, calls=%fused_computation | custom fusion | bytes 4198400 | tf_op jit(solution)/shard_map/gather | solution.py:36
  44.5 2.1 fusion.18
  46.6 5.0 convolution_convert_fusion
  51.6 2.6 copy.31
  54.2 1.8 copy.53
  57.0 6.2 gather_fusion.2
  63.4 1.6 fusion.65
  66.8 2.8 fusion.52
  70.3 10.2 %fusion.66 = f32[1,8192]{1,0:T(1,128)S(1)} fusion(bf16[8192,1024]{1,0:T(8,128)(2,1)} %copy.102, bf16[1024,1]{0,1:T(2,128)(2,1)S(1)} %reshape.200), kind=kOutput, calls=%fused_computation.113 | convolution fusion | flops 16777216 | bytes 16812032 | tf_op jit(solution)/shard_map/dot_general | solution.py:30
  81.1 6.1 gather_fusion.1
  87.3 14.4 %gather_fusion.3 = bf16[1024,1024]{1,0:T(8,128)(2,1)} fusion(bf16[8192,1024]{1,0:T(8,128)(2,1)} %copy.103, s32[1024]{0:T(1024)S(1)} %broadcast_clamp_fusion), kind=kCustom, calls=%fused_computation.3 | custom fusion | bytes 4198400 | tf_op jit(solution)/shard_map/gather | solution.py:37
  101.6 74.5 %all-reduce.8.cloned.1.call-done = f32[1024,1024]{1,0:T(8,128)} async-done(((f32[1024,1024]{1,0:T(8,128)}), f32[1024,1024]{1,0:T(8,128)}) %all-reduce.8.cloned.1.call-update) | async-done | bytes 4194320 | tf_op jit(solution)/shard_map/psum | solution.py:71
  176.1 3.5 multiply_reduce_fusion.2
  179.6 2.4 fusion.60
  183.3 5.2 fusion.13
  188.6 1.3 copy-done.34
  189.9 4.3 fusion.67
  194.7 7.6 fusion.61
  202.4 95.7 %all-reduce.10.cloned.1.call-done = f32[1024,1024]{1,0:T(8,128)} async-done(((f32[1024,1024]{1,0:T(8,128)}), f32[1024,1024]{1,0:T(8,128)}) %all-reduce.10.cloned.1.call-update) | async-done | bytes 4194320 | tf_op jit(solution)/shard_map/psum | solution.py:87
  298.0 4.6 multiply_reduce_fusion
  302.7 1.3 copy-done.5
  303.9 1.5 fusion.6
  305.5 1.3 copy-done.13
  306.8 1.6 convolution_convert_fusion.2
  308.4 2.8 reshape.202
  311.2 1.5 copy.38
  312.7 1.8 multiply_reduce_fusion.3
  319.8 3.9 fusion.30
  323.9 1.3 copy-done.35
  325.2 6.8 fusion.59
  332.1 5.1 fusion.42
  337.2 1.7 fusion.50
  338.9 3.7 fusion.28
  342.7 153.2 %all-reduce.14.cloned.1.call-done = (f32[1024,1024]{1,0:T(8,128)}, f32[1024,1024]{1,0:T(8,128)}) async-done(((f32[1024,1024]{1,0:T(8,128)}, f32[1024,1024]{1,0:T(8,128)}), (f32[1024,1024]{1,0:T(8,128)}, f32[1024,1024]{1,0:T(8,128)})) %all-reduce.14.cloned.1.call-update) | async-done | bytes 8388624 | tf_op jit(solution)/shard_map/psum | solution.py:76
  495.9 4.8 fusion.17
  501.3 1.9 fusion.5
  503.2 31.0 %all-reduce = (f32[1024]{0:T(1024)}, f32[1024]{0:T(1024)}, f32[1024]{0:T(1024)}, f32[]{:T(128)}, f32[]{:T(128)}) all-reduce(f32[1024]{0:T(1024)S(1)} %get-tuple-element.13, f32[1024]{0:T(1024)S(1)} %get-tuple-element.11, f32[1024]{0:T(1024)S(1)} %get-tuple-element.15, f32[]{:T(128)} %get-tuple-element.34, ...), channel_id=1, replica_groups=mesh['dp'=8,'mp'=4] {'dp'}, use_global_device_ids=true, to_apply=%region_15.16 | all-reduce | flops 3074 | bytes 24592 | tf_op jit(solution)/shard_map/psum | solution.py:129
  536.2 7.6 fusion.16
  543.9 21.8 %scatter_fusion = bf16[8192,1024]{1,0:T(8,128)(2,1)} fusion(bf16[8192,1024]{1,0:T(8,128)(2,1)} %copy.103, s32[1024]{0:T(1024)S(1)} %bitcast.98, bf16[1024,1024]{1,0:T(8,128)(2,1)} %fusion.16), kind=kCustom, calls=%fused_computation.5 | custom fusion | bytes 6295552 | tf_op jit(solution)/shard_map/scatter | solution.py:128
  565.7 23.0 %scatter_custom_fusion = bf16[8192,1024]{1,0:T(8,128)(2,1)} fusion(bf16[8192,1024]{1,0:T(8,128)(2,1)} %copy.102, s32[1024]{0:T(1024)S(1)} %bitcast.99, bf16[1024,1024]{1,0:T(8,128)(2,1)S(1)} %copy-done.2, f32[1024]{0:T(1024)S(1)} %gather_fusion.1, f32[1024,1024]{1,0:T(8,128)} %all-reduce.8.cloned.1.call-done, f32[1024,1024]{1,0:T(8,128)} %get-tuple-element.25), kind=kCustom, calls=%fused_computation.47 | custom fusion | flops 5242880 | bytes 27267072 | tf_op jit(solution)/shard_map/scatter | solution.py:80
  588.6 166.8 %all-reduce.12.cloned.1.call-done = (f32[1024,768]{1,0:T(8,128)}, f32[256,1024]{1,0:T(8,128)}, f32[1024,1024]{1,0:T(8,128)}, f32[1024,1024]{1,0:T(8,128)}) async-done(((f32[1024,768]{1,0:T(8,128)}, f32[256,1024]{1,0:T(8,128)}, f32[1024,1024]{1,0:T(8,128)}, f32[1024,1024]{1,0:T(8,128)}), (f32[1024,768]{1,0:T(8,128)}, f32[256,1024]{1,0:T(8,128)}, f32[1024,1024]{1,0:T(8,128)}, ...) | async-done | bytes 12582928 | tf_op jit(solution)/shard_map/psum | solution.py:129
  755.5 3.9 copy.104
  760.3 2.1 copy.106
  762.5 1.6 copy-done.15
  764.0 2.0 copy.107
  (103 shorter events, 13.3 us)
Async XLA Ops:
  7.2 172.4 %copy-start = (bf16[1024,1024]{1,0:T(8,128)(2,1)S(1)}, bf16[1024,1024]{1,0:T(8,128)(2,1)}, u32[]{:S(2)}) copy-start(bf16[1024,1024]{1,0:T(8,128)(2,1)} %param.20) | copy-start | bytes 6291460
  7.2 168.9 %all-reduce.8.cloned.1.call-start = ((), (), s32[]{:S(2)}) async-start(), calls=%async_computation | async-start | bytes 8388608 | tf_op jit(solution)/shard_map/psum | solution.py:71
  7.2 17.0 %copy-start.11 = (bf16[8192,1024]{1,0:T(8,128)(2,1)S(1)}, bf16[8192,1024]{1,0:T(8,128)(2,1)}, u32[]{:S(2)}) copy-start(bf16[8192,1024]{1,0:T(8,128)(2,1)} %param.14) | copy-start | bytes 50331652
  24.2 6.2 copy-start.27
  30.5 16.0 %copy-start.28 = (bf16[1024]{0:T(1024)(128)(2,1)S(1)}, bf16[1024]{0:T(1024)(128)(2,1)}, u32[]{:S(2)}) copy-start(bf16[1024]{0:T(1024)(128)(2,1)} %param.15) | copy-start | bytes 6148
  51.6 5.4 copy-start.25
  57.0 8.4 %copy-start.18 = (bf16[8,128,4,1,64]{1,0,4,3,2:T(8,128)(2,1)}, bf16[8,128,4,1,64]{1,0,4,3,2:T(8,128)(2,1)S(1)}, u32[]{:S(2)}) copy-start(bf16[8,128,4,1,64]{1,0,4,3,2:T(8,128)(2,1)S(1)} %get-tuple-element.32) | copy-start | bytes 1572868
  57.0 8.4 %copy-start.17 = (bf16[8,128,4,1,64]{1,0,4,3,2:T(8,128)(2,1)}, bf16[8,128,4,1,64]{1,0,4,3,2:T(8,128)(2,1)S(1)}, u32[]{:S(2)}) copy-start(bf16[8,128,4,1,64]{1,0,4,3,2:T(8,128)(2,1)S(1)} %get-tuple-element.31) | copy-start | bytes 1572868
  65.0 1.3 copy-start.9
  65.5 1.4 copy-start.24
  69.6 0.7 copy-start.29
  69.6 0.7 copy-start.26
  69.6 228.4 %all-reduce.10.cloned.1.call-start = ((), (), s32[]{:S(2)}) async-start(), calls=%async_computation.1 | async-start | bytes 8388608 | tf_op jit(solution)/shard_map/psum | solution.py:87
  179.6 2.5 copy-start.3
  179.6 3.1 copy-start.6
  179.6 3.7 copy-start.30
  183.3 5.2 copy-start.32
  188.6 1.3 copy-start.34
  194.2 301.6 %all-reduce.14.cloned.1.call-start = ((), (), s32[]{:S(2)}) async-start(), calls=%async_computation.3 | async-start | bytes 16777216 | tf_op jit(solution)/shard_map/psum | solution.py:76
  194.7 108.0 %copy-start.7 = (bf16[1024,1024]{1,0:T(8,128)(2,1)S(1)}, bf16[1024,1024]{1,0:T(8,128)(2,1)}, u32[]{:S(2)}) copy-start(bf16[1024,1024]{1,0:T(8,128)(2,1)} %gather_fusion.3) | copy-start | bytes 6291460
  298.0 4.7 copy-start.4
  298.0 5.9 copy-start.5
  305.5 1.4 copy-start.13
  306.8 5.8 copy-start.10
  312.7 2.4 copy-start.20
  314.5 1.0 copy-start.19
  316.3 3.4 copy-start.31
  318.6 1.1 copy-start.21
  323.6 1.6 copy-start.35
  323.7 431.8 %all-reduce.12.cloned.1.call-start = ((), (), s32[]{:S(2)}) async-start(), calls=%async_computation.2 | async-start | bytes 25165824 | tf_op jit(solution)/shard_map/psum | solution.py:129
  325.2 6.8 copy-start.8
  325.2 6.8 copy-start.33
  332.1 5.1 copy-start.14
  332.1 6.8 copy-start.2
  332.1 6.8 copy-start.22
  495.9 5.4 copy-start.12
  755.5 3.9 copy-start.23
  755.5 4.9 copy-start.16
  760.3 3.7 copy-start.15
  760.3 5.7 copy-start.1
Sparse Core Ops, SparseCore 0:
  69.7 106.3 all-reduce.7
  194.4 103.6 all-reduce.9
  323.8 172.0 all-reduce.13
  499.5 255.9 all-reduce.11
where the time goes:
time: 783 us; the launch traced here: 775 us
  waiting for transfers between devices  490 us (63%)
  local copies, waits for them, and re-layouts  116 us (15%)
  matrix products  66.4 us (8%)
  other arithmetic  51.8 us (7%)
  blocking collectives  31 us (4%)
  between operations  19 us (2%)
    psum x1, waiting for transfers between devices, shards(): lax.psum((grad_gain_attn, grad_gain_mlp, grad_router, grad_qkv, grad_out,...  167 us
    psum x1, waiting for transfers between devices, shards(): lax.psum(jnp.dot(hidden, w_down, preferred_element_type=jnp.float32), 'mp')  153 us
    psum x1, waiting for transfers between devices, shards(): lax.psum(jnp.dot(grad_pre, w_up.T, preferred_element_type=jnp.float32), '...  95.7 us
    psum x1, waiting for transfers between devices, shards(): lax.psum(jnp.dot(heads_out, w_out, preferred_element_type=jnp.float32), '...  74.5 us
    unnamed x81, local copies, waits for them, and re-layouts  44.3 us
    psum x1, blocking collectives, shards(): lax.psum((grad_gain_attn, grad_gain_mlp, grad_router, grad_qkv, grad_out,...  31 us
    scatter x1, other arithmetic, shards(): output = tokens.at[picks].set(updated_low)  23 us
    scatter x1, local copies, waits for them, and re-layouts, shards(): grad_tokens = cotangent.at[picks].set(grad_rows_low)  21.8 us
  transfers between devices with their start and end apart: 4, of which 4 were waited for; matrix products, arithmetic and copies ran while one was open for 15% of the time, Pallas kernels for 0%

commit v1 on v0

v1 whole, which is shorter than its diff:
```python
import functools

import jax
import jax.numpy as jnp
from jax import lax
from jax.experimental import pallas as pl
from jax.experimental.pallas import tpu as pltpu
from jax.sharding import PartitionSpec as P

HD = 64
EPS = 1e-06
SCALE = HD ** (-0.5)
GELU_C = (2.0 / 3.141592653589793) ** 0.5
GELU_A = 0.044715
F32 = jnp.float32
BF16 = jnp.bfloat16


def dot(left, right, on=((1,), (0,))):
    return lax.dot_general(left, right, (on, ((), ())), preferred_element_type=F32)


NT = ((1,), (1,))
TN = ((0,), (0,))


def iota(shape, axis):
    return lax.broadcasted_iota(jnp.int32, shape, axis)


def sigmoid(value):
    return 1.0 / (1.0 + jnp.exp(-value))


def call(body, grid, in_specs, out_specs, out_shape, flops, nbytes, name, scratch=(), alias=None):
    return pl.pallas_call(
        body,
        grid_spec=pltpu.PrefetchScalarGridSpec(
            num_scalar_prefetch=1,
            grid=grid,
            in_specs=in_specs,
            out_specs=out_specs,
            scratch_shapes=list(scratch),
        ),
        out_shape=out_shape,
        cost_estimate=pl.CostEstimate(
            flops=int(flops), bytes_accessed=int(nbytes), transcendentals=0
        ),
        input_output_aliases=alias or {},
        name=name,
    )


def whole(shape):
    zeros = (0,) * len(shape)
    return pl.BlockSpec(shape, lambda *_: zeros)


def one_hot_rows(routes_row, length):
    routed = routes_row.shape[1]
    eye = iota((routed, routed), 0) == iota((routed, routed), 1)
    column = jnp.sum(jnp.where(eye, routes_row.astype(F32), 0.0), axis=1, keepdims=True)
    return iota((routed, length), 1) == column.astype(jnp.int32), eye


def head_mask(hot, eye, seg_line):
    seg_col = jnp.sum(jnp.where(hot, seg_line, 0.0), axis=1, keepdims=True)
    seg_row = jnp.sum(jnp.where(eye, seg_col, 0.0), axis=0, keepdims=True)
    routed = eye.shape[0]
    causal = iota((routed, routed), 0) >= iota((routed, routed), 1)
    return causal & (seg_col == seg_row)


def softmax_head(query, key, allowed):
    logits = jnp.where(allowed, dot(query, key, NT) * SCALE, -1e30)
    expon = jnp.exp(logits - jnp.max(logits, axis=1, keepdims=True))
    return expon / jnp.sum(expon, axis=1, keepdims=True)


def front_body(
    heads, slice_rows, where, tokens, routes, segments, gain, router, w_qkv,
    xr_out, a1_out, qkv_out, mask_out, mixed_out, score_out,
):
    step = pl.program_id(0)
    length = tokens.shape[0]
    hot, eye = one_hot_rows(routes[pl.ds(step, 1), :], length)
    seg_line = segments[pl.ds(step, 1), :].astype(F32)
    allowed = head_mask(hot, eye, seg_line)
    mask_out[...] = jnp.where(allowed, 1.0, 0.0).astype(BF16)
    rows = dot(jnp.where(hot, 1.0, 0.0).astype(BF16), tokens[...])
    xr_out[...] = rows.astype(BF16)
    vec = router[...].astype(F32)
    start = pl.multiple_of(where[0] * slice_rows, slice_rows)
    part = tokens[pl.ds(start, slice_rows), :].astype(F32)
    total = jnp.sum(sigmoid(jnp.sum(part * vec, axis=1, keepdims=True)), axis=0, keepdims=True)
    chosen = jnp.sum(sigmoid(jnp.sum(rows * vec, axis=1, keepdims=True)), axis=0, keepdims=True)

    @pl.when(step == 0)
    def _():
        score_out[...] = jnp.zeros_like(score_out)

    which = iota(score_out.shape, 0)
    score_out[...] += jnp.where(which == 0, total, jnp.where(which == 1, chosen, 0.0))
    inverse = lax.rsqrt(jnp.mean(rows * rows, axis=1, keepdims=True) + EPS)
    normed = (rows * inverse * gain[...].astype(F32)).astype(BF16)
    a1_out[...] = normed
    joint = dot(normed, w_qkv[...]).astype(BF16)
    qkv_out[...] = joint
    for head in range(heads):
        base = head * 3 * HD
        query = joint[:, base : base + HD]
        key = joint[:, base + HD : base + 2 * HD]
        value = joint[:, base + 2 * HD : base + 3 * HD]
        probs = softmax_head(query, key, allowed).astype(BF16)
        mixed_out[:, head * HD : (head + 1) * HD] = dot(probs, value).astype(BF16)


def cot_body(where, cotangent, routes, xr, router, w_down, dyr_out, gm_out, dh_out):
    step = pl.program_id(0)
    hot, _ = one_hot_rows(routes[pl.ds(step, 1), :], cotangent.shape[0])
    rows = dot(jnp.where(hot, 1.0, 0.0).astype(BF16), cotangent[...])
    dyr_out[...] = rows.astype(BF16)
    vec = router[...].astype(F32)
    rate = sigmoid(jnp.sum(xr[...].astype(F32) * vec, axis=1, keepdims=True))
    low = (rate * rows).astype(BF16)
    gm_out[...] = low
    dh_out[...] = dot(low, w_down[...], NT)


def middle_body(parts, table, *refs):
    mixed = refs[:parts]
    w_out, xr, dh, gain, w_up = refs[parts : parts + 5]
    attn_out, a2_out, hid_out, du_out, da2_out, gain_out = refs[parts + 5 :]
    attn = dot(mixed[0][...], w_out[0])
    for part in range(1, parts):
        attn = attn + dot(mixed[part][...], w_out[part])
    attn_out[...] = attn
    y = xr[...].astype(F32) + attn
    scaled = y * lax.rsqrt(jnp.mean(y * y, axis=1, keepdims=True) + EPS)
    a2 = (scaled * gain[...].astype(F32)).astype(BF16)
    a2_out[...] = a2
    u = dot(a2, w_up[...])
    square = u * u
    t = jnp.tanh(GELU_C * (u + GELU_A * (u * square)))
    hid_out[...] = (0.5 * u * (1.0 + t)).astype(BF16)
    slope = 0.5 * (1.0 + t) + (0.5 * GELU_C) * u * (1.0 - t * t) * (1.0 + 3.0 * GELU_A * square)
    du = (dh[...] * slope).astype(BF16)
    du_out[...] = du
    da2 = dot(du, w_up[...], NT)
    da2_out[0] = da2.astype(BF16)

    @pl.when(pl.program_id(0) == 0)
    def _():
        gain_out[...] = jnp.zeros_like(gain_out)

    gain_out[...] += jnp.sum((da2 * scaled).reshape(-1, 8, da2.shape[1]), axis=0)


def rows_body(parts, where, *refs):
    pieces = refs[:parts]
    attn, xr, dyr, gain, router, w_out = refs[parts : parts + 6]
    dyn_out, ga_out, do_out = refs[parts + 6 :]
    da2 = pieces[0][...].astype(F32)
    for piece in pieces[1:]:
        da2 = da2 + piece[...].astype(F32)
    rows = xr[...].astype(F32)
    y = rows + attn[...]
    inverse = lax.rsqrt(jnp.mean(y * y, axis=1, keepdims=True) + EPS)
    t = gain[...].astype(F32) * da2
    scaled = y * inverse
    dyn = inverse * (t - scaled * jnp.mean(t * scaled, axis=1, keepdims=True))
    dyn_out[...] = dyn
    rate = sigmoid(jnp.sum(rows * router[...].astype(F32), axis=1, keepdims=True))
    ga = (rate * dyr[...].astype(F32) + dyn).astype(BF16)
    ga_out[...] = ga
    for part in range(parts):
        do_out[part] = dot(ga, w_out[part], NT).astype(BF16)


def delta_body(parts, where, *refs):
    pieces = refs[:parts]
    attn, xr, dyr, dyn, router = refs[parts : parts + 5]
    upd_out, base_out, grad_router_out = refs[parts + 5 :]
    delta = attn[...]
    for piece in pieces:
        delta = delta + piece[...].astype(F32)
    rows = xr[...].astype(F32)
    grads = dyr[...].astype(F32)
    vec = router[...].astype(F32)
    rate = sigmoid(jnp.sum(rows * vec, axis=1, keepdims=True))
    upd_out[...] = (rows + rate * delta).astype(BF16)
    dlogit = jnp.sum(grads * delta, axis=1, keepdims=True) * rate * (1.0 - rate)
    base_out[...] = grads + dyn[...] + dlogit * vec

    @pl.when(pl.program_id(0) == 0)
    def _():
        grad_router_out[...] = jnp.zeros_like(grad_router_out)

    grad_router_out[...] += jnp.sum((dlogit * rows).reshape(-1, 8, rows.shape[1]), axis=0)


def back_body(heads, where, qkv, mask, dmixed, xr, gain, w_qkv, dqkv_out, da1_out, gain_out):
    joint = qkv[...]
    allowed = mask[...].astype(F32) > 0.5
    grads = dmixed[0]
    pieces = []
    for head in range(heads):
        base = head * 3 * HD
        query = joint[:, base : base + HD]
        key = joint[:, base + HD : base + 2 * HD]
        value = joint[:, base + 2 * HD : base + 3 * HD]
        dmix = grads[:, head * HD : (head + 1) * HD]
        probs = softmax_head(query, key, allowed)
        dprobs = dot(dmix, value, NT)
        spread = jnp.sum(probs * dprobs, axis=1, keepdims=True)
        dlog = (probs * (dprobs - spread)).astype(BF16)
        dquery = dot(dlog, key) * SCALE
        dkey = dot(dlog, query, TN) * SCALE
        dvalue = dot(probs.astype(BF16), dmix, TN)
        pieces += [dquery.astype(BF16), dkey.astype(BF16), dvalue.astype(BF16)]
    for at, piece in enumerate(pieces):
        dqkv_out[:, at * HD : (at + 1) * HD] = piece
    da1 = dot(dqkv_out[...], w_qkv[...], NT)
    da1_out[0] = da1.astype(BF16)
    rows = xr[...].astype(F32)
    scaled = rows * lax.rsqrt(jnp.mean(rows * rows, axis=1, keepdims=True) + EPS)

    @pl.when(pl.program_id(0) == 0)
    def _():
        gain_out[...] = jnp.zeros_like(gain_out)

    gain_out[...] += jnp.sum((da1 * scaled).reshape(-1, 8, da1.shape[1]), axis=0)


def last_body(parts, where, *refs):
    pieces = refs[:parts]
    xr, base, gain = refs[parts : parts + 3]
    (out,) = refs[parts + 3 :]
    da1 = pieces[0][...].astype(F32)
    for piece in pieces[1:]:
        da1 = da1 + piece[...].astype(F32)
    rows = xr[...].astype(F32)
    inverse = lax.rsqrt(jnp.mean(rows * rows, axis=1, keepdims=True) + EPS)
    t = gain[...].astype(F32) * da1
    scaled = rows * inverse
    dxn = inverse * (t - scaled * jnp.mean(t * scaled, axis=1, keepdims=True))
    out[...] = (base[...] + dxn).astype(BF16)


def put_body(where, source, routes, rows, *refs):
    out = refs[-1]
    length = source.shape[0]
    at = where[pl.program_id(0)]
    line = routes[pl.ds(at, 1), :]
    hot = iota((length, line.shape[1]), 0) == line
    picked = jnp.where(hot, 1.0, 0.0)
    taken = jnp.sum(picked, axis=1, keepdims=True) > 0.5
    moved = dot(picked.astype(BF16), rows[...])
    out[...] = jnp.where(taken, moved, source[...].astype(F32)).astype(BF16)


def put_rows(source, routes, rows, order, target, name):
    seqs, routed = routes.shape
    length = source.shape[0] // seqs
    width = source.shape[1]
    count = rows.shape[0] // routed
    in_specs = [
        pl.BlockSpec((length, width), lambda i, w: (w[i], 0)),
        whole(routes.shape),
        pl.BlockSpec((routed, width), lambda i, w: (i, 0)),
    ]
    args = [order, source, routes, rows]
    alias = None
    if target is not None:
        in_specs.append(pl.BlockSpec(memory_space=pl.ANY))
        args.append(target)
        alias = {4: 0}
    return call(
        put_body,
        (count,),
        in_specs,
        pl.BlockSpec((length, width), lambda i, w: (w[i], 0)),
        jax.ShapeDtypeStruct(source.shape, BF16),
        2 * count * length * routed * width,
        count * length * width * 4,
        name,
        alias=alias,
    )(*args)


def swap(value, axis, offset):
    size = lax.axis_size(axis)
    return lax.ppermute(value, axis, [(i, i ^ offset) for i in range(size)])


def block_of(value, index, rows):
    return lax.dynamic_slice_in_dim(value, index * rows, rows, 0)


def in_core_order(core, mine, other):
    return jnp.where(
        core == 0,
        jnp.concatenate([mine, other], axis=0),
        jnp.concatenate([other, mine], axis=0),
    )


def line_sum(value, depth):
    at = lax.axis_index("dp") // 2
    half = depth // 2

    def shift(array, pairs):
        return lax.ppermute(
            array, "dp", [(2 * a + c, 2 * b + c) for a, b in pairs for c in range(2)]
        )

    def mirrored(a, b):
        return [(a, b), (depth - 1 - a, depth - 1 - b)]

    for step in range(half - 1):
        got = shift(value, mirrored(step, step + 1))
        value = (value.astype(F32) + got.astype(F32)).astype(BF16)
    if depth > 1:
        got = shift(value, mirrored(half - 1, half))
        value = (value.astype(F32) + got.astype(F32)).astype(BF16)
    for step in reversed(range(half - 1)):
        got = shift(value, mirrored(step + 1, step))
        here = (at == step) | (at == depth - 1 - step)
        value = jnp.where(here, got, value)
    return value


def core_half(value, core):
    half = value.shape[0] // 2
    keep = block_of(value, core, half)
    give = block_of(value, 1 - core, half)
    got = swap(give.astype(BF16), "dp", 1)
    return (keep.astype(F32) + got.astype(F32)).astype(BF16)


def core_join(value, core):
    return in_core_order(core, value, swap(value, "dp", 1)).astype(F32)


def shards(
    tokens, segments, routes, cotangent, gain_attn, gain_mlp, w_router, w_qkv, w_out, w_up, w_down
):
    seqs, length = segments.shape
    routed = routes.shape[1]
    width = tokens.shape[1]
    total = seqs * routed
    wide = w_out.shape[0]
    heads = wide // HD
    joint = w_qkv.shape[1]
    hidden = w_up.shape[1]
    parts = lax.axis_size("mp")
    depth = lax.axis_size("dp") // 2
    own = total // parts
    rank = lax.axis_index("mp")
    core = lax.axis_index("dp") % 2
    aligned = own % routed == 0
    per = own // routed if aligned else 1
    where = rank.reshape(1).astype(jnp.int32)
    gain_one = gain_attn.reshape(1, width)
    gain_two = gain_mlp.reshape(1, width)
    router = w_router.reshape(1, width)
    partners = list(range(1, parts))
    sds = jax.ShapeDtypeStruct

    share = block_of(w_out, core, wide // 2)
    mine = jnp.stack([swap(share, "mp", j) for j in partners])
    other = swap(mine, "dp", 1)
    w_all = jnp.where(
        core == 0,
        jnp.concatenate([mine, other], axis=1),
        jnp.concatenate([other, mine], axis=1),
    )
    w_all = jnp.concatenate([w_out[None], w_all], axis=0)

    xr, a1, qkv, mask, mixed, score = call(
        functools.partial(front_body, heads, length // parts),
        (seqs,),
        [
            pl.BlockSpec((length, width), lambda i, w: (i, 0)),
            whole(routes.shape),
            whole(segments.shape),
            whole((1, width)),
            whole((1, width)),
            whole(w_qkv.shape),
        ],
        [
            pl.BlockSpec((routed, width), lambda i, w: (i, 0)),
            pl.BlockSpec((routed, width), lambda i, w: (i, 0)),
            pl.BlockSpec((routed, joint), lambda i, w: (i, 0)),
            pl.BlockSpec((routed, routed), lambda i, w: (i, 0)),
            pl.BlockSpec((routed, wide), lambda i, w: (i, 0)),
            whole((8, 128)),
        ],
        [
            sds((total, width), BF16),
            sds((total, width), BF16),
            sds((total, joint), BF16),
            sds((total, routed), BF16),
            sds((total, wide), BF16),
            sds((8, 128), F32),
        ],
        2 * total * width * (length + joint) * 1.3,
        2 * seqs * length * width + 8 * total * width,
        "front",
    )(where, tokens, routes, segments, gain_one, router, w_qkv)

    mixed_all = [mixed] + [swap(mixed, "mp", j) for j in partners]

    dyr, gm, dh = call(
        cot_body,
        (seqs,),
        [
            pl.BlockSpec((length, width), lambda i, w: (i, 0)),
            whole(routes.shape),
            pl.BlockSpec((routed, width), lambda i, w: (i, 0)),
            whole((1, width)),
            whole(w_down.shape),
        ],
        [
            pl.BlockSpec((routed, width), lambda i, w: (i, 0)),
            pl.BlockSpec((routed, width), lambda i, w: (i, 0)),
            pl.BlockSpec((routed, hidden), lambda i, w: (i, 0)),
        ],
        [sds((total, width), BF16), sds((total, width), BF16), sds((total, hidden), F32)],
        2 * total * width * (length + hidden),
        2 * seqs * length * width + 6 * total * width + 4 * total * hidden,
        "cot",
    )(where, cotangent, routes, xr, router, w_down)

    order = partners[::-1] + [0]
    tile = min(own, 128)
    tiles = own // tile
    blocks = jnp.stack([rank ^ j for j in order])
    table = (blocks[:, None] * tiles + jnp.arange(tiles)[None, :]).reshape(-1).astype(jnp.int32)

    def by_row(i, t):
        return (t[i], 0)

    steps = parts * tiles
    attn, a2, hid, du, da2, gain_two_part = call(
        functools.partial(middle_body, parts),
        (steps,),
        [pl.BlockSpec((tile, wide), by_row)] * parts
        + [
            whole(w_all.shape),
            pl.BlockSpec((tile, width), by_row),
            pl.BlockSpec((tile, hidden), by_row),
            whole((1, width)),
            whole(w_up.shape),
        ],
        [
            pl.BlockSpec((tile, width), lambda i, t: (jnp.maximum(i - (steps - tiles), 0), 0)),
            pl.BlockSpec((tile, width), by_row),
            pl.BlockSpec((tile, hidden), by_row),
            pl.BlockSpec((tile, hidden), by_row),
            pl.BlockSpec((1, tile, width), lambda i, t: (i // tiles, i % tiles, 0)),
            whole((8, width)),
        ],
        [
            sds((own, width), F32),
            sds((total, width), BF16),
            sds((total, hidden), BF16),
            sds((total, hidden), BF16),
            sds((parts, own, width), BF16),
            sds((8, width), F32),
        ],
        2 * total * width * (parts * wide + 2 * hidden),
        total * (10 * width + 8 * hidden) + 2 * width * (hidden + parts * wide),
        "middle",
    )(table, *mixed_all, w_all, xr, dh, gain_two, w_up)

    da2_all = [da2[-1]] + [swap(da2[at], "mp", j) for at, j in enumerate(order[:-1])]

    mlp = dot(hid, w_down).astype(BF16)
    grad_up = dot(a2, du, TN).astype(BF16)
    grad_down = dot(hid, gm, TN).astype(BF16)
    mlp_all = [block_of(mlp, rank, own)] + [
        swap(block_of(mlp, rank ^ j, own), "mp", j) for j in partners
    ]

    own_tiles = lambda i, w: (w[0] * tiles + i, 0)
    flat = lambda i, w: (i, 0)
    row_block = pl.BlockSpec((tile, width), flat)
    own_block = pl.BlockSpec((tile, width), own_tiles)
    dyn, ga, dmix = call(
        functools.partial(rows_body, parts),
        (tiles,),
        [row_block] * parts
        + [row_block, own_block, own_block, whole((1, width)), whole((1, width)), whole(w_all.shape)],
        [row_block, row_block, pl.BlockSpec((parts, tile, wide), lambda i, w: (0, i, 0))],
        [sds((own, width), F32), sds((own, width), BF16), sds((parts, own, wide), BF16)],
        2 * own * width * parts * wide,
        own * width * 24 + 2 * width * width,
        "rows",
    )(where, *da2_all, attn, xr, dyr, gain_two, router, w_all)

    dmix_all = jnp.stack([dmix[0]] + [swap(dmix[j], "mp", j) for j in partners])

    upd, base, router_part = call(
        functools.partial(delta_body, parts),
        (tiles,),
        [row_block] * parts + [row_block, own_block, own_block, row_block, whole((1, width))],
        [row_block, row_block, whole((8, width))],
        [sds((own, width), BF16), sds((own, width), F32), sds((8, width), F32)],
        own * width * 20,
        own * width * 24,
        "delta",
    )(where, *mlp_all, attn, xr, dyr, dyn, router)
    upd_all = [upd] + [swap(upd, "mp", j) for j in partners]

    if aligned:
        by_owner = lambda i, w: ((i // per) ^ w[0], i % per, 0)
        da1_shape = (parts, own, width)
    else:
        dmix_all = dmix_all[jnp.arange(parts) ^ rank].reshape(1, total, wide)
        by_owner = lambda i, w: (0, i, 0)
        da1_shape = (1, total, width)
    dqkv, da1, gain_one_part = call(
        functools.partial(back_body, heads),
        (seqs,),
        [
            pl.BlockSpec((routed, joint), flat),
            pl.BlockSpec((routed, routed), flat),
            pl.BlockSpec((1, routed, wide), by_owner),
            pl.BlockSpec((routed, width), flat),
            whole((1, width)),
            whole(w_qkv.shape),
        ],
        [
            pl.BlockSpec((routed, joint), flat),
            pl.BlockSpec((1, routed, width), by_owner),
            whole((8, width)),
        ],
        [sds((total, joint), BF16), sds(da1_shape, BF16), sds((8, width), F32)],
        2 * total * width * joint * 1.5,
        total * (4 * joint + 6 * width) + 2 * width * joint,
        "back",
    )(where, qkv, mask, dmix_all, xr, gain_one, w_qkv)

    if aligned:
        da1_blocks = [da1[j] for j in range(parts)]
    else:
        da1_blocks = [block_of(da1[0], rank ^ j, own) for j in range(parts)]
    da1_all = [da1_blocks[0]] + [swap(da1_blocks[j], "mp", j) for j in partners]

    grad_qkv = dot(a1, dqkv, TN).astype(BF16)

    last = call(
        functools.partial(last_body, parts),
        (tiles,),
        [row_block] * parts + [own_block, row_block, whole((1, width))],
        row_block,
        sds((own, width), BF16),
        own * width * 20,
        own * width * 18,
        "last",
    )(where, *da1_all, xr, base, gain_one)
    last_all = [last] + [swap(last, "mp", j) for j in partners]

    def spread(source, rows_all, name):
        if not aligned:
            rows = jnp.stack(rows_all)[jnp.arange(parts) ^ rank].reshape(total, width)
            return put_rows(source, routes, rows, jnp.arange(seqs, dtype=jnp.int32), None, name)
        target = None
        for j, rows in enumerate(rows_all):
            seq = ((rank ^ j) * per + jnp.arange(per)).astype(jnp.int32)
            target = put_rows(source, routes, rows, seq, target, name)
        return target

    output = spread(tokens, upd_all, "put_out")
    grad_tokens = spread(cotangent, last_all, "put_grad")

    grad_up = core_join(line_sum(core_half(grad_up, core), depth), core)
    grad_down = core_join(line_sum(core_half(grad_down, core), depth), core)
    grad_qkv = core_join(line_sum(core_half(grad_qkv, core), depth), core)

    def out_part(j):
        rows = block_of(mixed_all[j], rank, own)
        return dot(rows, ga, TN).astype(BF16)

    outs = jnp.stack([out_part(j) for j in range(parts)], axis=1)
    outs = core_half(outs, core)
    half = outs[:, 0].astype(F32)
    for j in partners:
        half = half + swap(outs[:, j], "mp", j).astype(F32)
    grad_out = core_join(line_sum(half.astype(BF16), depth), core)

    lines = jnp.sum(
        jnp.stack([gain_one_part, gain_two_part, router_part]), axis=1
    )
    scores = jnp.concatenate(
        [score[0:1] / 1.0, score[1:2] / parts, jnp.zeros((6, 128), F32)], axis=0
    ).reshape(1, -1)
    scores = jnp.pad(scores, ((0, 0), (0, width - 1024))) if width > 1024 else scores[:, :width]
    small = jnp.concatenate([lines, scores, jnp.zeros((4, width), F32)], axis=0)
    bit = 1
    while bit < 2 * depth:
        small = small + swap(small, "dp", bit)
        bit *= 2
    bit = 1
    while bit < parts:
        small = small + swap(small, "mp", bit)
        bit *= 2
    score_total = small[3, 0]
    routed_total = small[3, 128]
    token_count = seqs * length * lax.axis_size("dp")
    return (
        output,
        grad_tokens,
        small[0],
        small[1],
        small[2],
        grad_qkv,
        grad_out,
        grad_up,
        grad_down,
        routed_total / score_total,
        score_total / token_count,
    )


def solution(mesh):
    rows = P("dp", None)
    columns = P(None, "mp")
    lines = P("mp", None)
    in_specs = (rows, rows, rows, rows, P(), P(), P(), columns, lines, columns, lines)
    out_specs = (rows, rows, P(), P(), P(), columns, lines, columns, lines, P(), P())
    return jax.shard_map(shards, mesh=mesh, in_specs=in_specs, out_specs=out_specs, check_vma=False)
```

time: 783 us -> 390 us (0.50)
  waiting for transfers between devices: 490 us -> 114 us
  Pallas kernels: 0 us -> 135 us
  local copies, waits for them, and re-layouts: 116 us -> 21.2 us
  starting transfers between devices: 0.95 us -> 54 us
  matrix products: 66.4 us -> 17.6 us
  blocking collectives: 31 us -> 0 us
  between operations: 19 us -> 5.61 us
  other arithmetic: 51.8 us -> 39 us
    psum x4 -> x0, waiting for transfers between devices: 490 us -> none  [the longest x1 167 us: shards(): lax.psum((grad_gain_attn, grad_gain_mlp, grad_router, grad_qkv, grad_out,...]
    pallas_call x0 -> x15, Pallas kernels: none -> 135 us  [the longest x8 40.5 us: put_rows(): call(put_body, (count,), in_specs, pl.BlockSpec((length, width), lambda i...]
    ppermute x0 -> x53, waiting for transfers between devices: none -> 114 us  [the longest x12 75.8 us: shift(): lax.ppermute(array, 'dp', [(2 * a + c, 2 * b + c) for a, b in pairs for c...]
    ppermute x0 -> x53, starting transfers between devices: none -> 54 us  [the longest x41 37.9 us: swap(): return lax.ppermute(value, axis, [(i, i ^ offset) for i in range(size)])]
    dot_general x19 -> x8, matrix products: 66.4 us -> 17.6 us  [dot(): lax.dot_general(left, right, (on, ((), ())), preferred_element_type=F32)]
    gather x4 -> x0, local copies, waits for them, and re-layouts: 40.6 us -> none  [the longest x1 14.4 us: shards(): grad_rows = cotangent[picks].astype(jnp.float32)]
    unnamed x81 -> x58, local copies, waits for them, and re-layouts: 44.3 us -> 6.45 us
    psum x1 -> x0, blocking collectives: 31 us -> none  [shards(): lax.psum((grad_gain_attn, grad_gain_mlp, grad_router, grad_qkv, grad_out,...]
  transfers between devices with their start and end apart: 4 -> 53, of which waited for: 4 -> 14; matrix products, arithmetic and copies ran while one was open for 15% -> 17% of each run, Pallas kernels for 0% -> 29%
where the time goes in v1:
time: 390 us; the launch traced here: 386 us
  Pallas kernels  135 us (35%)
  waiting for transfers between devices  114 us (29%)
  starting transfers between devices  54 us (14%)
  other arithmetic  39 us (10%)
  local copies, waits for them, and re-layouts  21.2 us (5%)
  matrix products  17.6 us (5%)
  between operations  5.61 us (1%)
    ppermute x12, waiting for transfers between devices, shift(): lax.ppermute(array, 'dp', [(2 * a + c, 2 * b + c) for a, b in pairs for c...  75.8 us
    pallas_call x8, Pallas kernels, put_rows(): call(put_body, (count,), in_specs, pl.BlockSpec((length, width), lambda i...  40.5 us
    ppermute x41, waiting for transfers between devices, swap(): return lax.ppermute(value, axis, [(i, i ^ offset) for i in range(size)])  38 us
    ppermute x41, starting transfers between devices, swap(): return lax.ppermute(value, axis, [(i, i ^ offset) for i in range(size)])  37.9 us
    pallas_call x1, Pallas kernels, shards(): call(functools.partial(back_body, heads), (seqs,), [pl.BlockSpec((routed,...  23.5 us
    pallas_call x1, Pallas kernels, shards(): call(functools.partial(front_body, heads, length // parts), (seqs,), [pl....  22.2 us
    pallas_call x1, Pallas kernels, shards(): call(functools.partial(middle_body, parts), (steps,), [pl.BlockSpec((tile...  21.3 us
    dot_general x8, matrix products, dot(): lax.dot_general(left, right, (on, ((), ())), preferred_element_type=F32)  17.6 us
  transfers between devices with their start and end apart: 53, of which 14 were waited for; matrix products, arithmetic and copies ran while one was open for 17% of the time, Pallas kernels for 29%

profile of v1, /device:TPU:0, one launch (start us, length us, event | category | flops | bytes accessed | tf_op | source)
XLA Modules:
  0.0 386.3 jit_solution(9652582246759274154)
XLA Ops:
  1.6 3.0 collective-permute-start.3
  8.8 22.2 %front.1 = (bf16[1024,1024]{1,0:T(8,128)(2,1)}, bf16[1024,1024]{1,0:T(8,128)(2,1)}, bf16[1024,768]{1,0:T(8,128)(2,1)}, bf16[1024,128]{1,0:T(8,128)(2,1)}, bf16[1024,256]{1,0:T(8,128)(2,1)}, /*index=5*/f32[8,128]{1,0:T(8,128)}) custom-call(s32[1]{0:T(128)} %bitcast.where, bf16[8192,1024]{1,0:T(8,128)(2,1)} %source.11, s32[8,128]{1,0:T(8,128)} %routes.19, ...), custom_call_target="tpu_custom_call" | custom-call | flops 4885525504 | bytes 25165824 | tf_op jit(solution)/shard_map/front/pallas_call | solution.py:380
  30.9 2.0 collective-permute-start
  36.3 15.2 %cot.1 = (bf16[1024,1024]{1,0:T(8,128)(2,1)}, bf16[1024,1024]{1,0:T(8,128)(2,1)}, f32[1024,1024]{1,0:T(8,128)}) custom-call(s32[1]{0:T(128)} %bitcast.where, bf16[8192,1024]{1,0:T(8,128)(2,1)} %source.15, s32[8,128]{1,0:T(8,128)} %routes.19, bf16[1024,1024]{1,0:T(8,128)(2,1)} %get-tuple-element.36.xr.refs_5_.refs_4_, ...), custom_call_target="tpu_custom_call" | custom-call | flops 4294967296 | bytes 27262976 | tf_op jit(solution)/shard_map/cot/pallas_call | solution.py:414
  57.7 21.3 %middle.1 = (f32[256,1024]{1,0:T(8,128)}, bf16[1024,1024]{1,0:T(8,128)(2,1)}, bf16[1024,1024]{1,0:T(8,128)(2,1)}, bf16[1024,1024]{1,0:T(8,128)(2,1)}, bf16[4,256,1024]{2,1,0:T(8,128)(2,1)}, /*index=5*/f32[8,1024]{1,0:T(8,128)}) custom-call(s32[8]{0:T(128)} %add.152.table, bf16[1024,256]{1,0:T(8,128)(2,1)} %get-tuple-element.35.refs_0_, ...), custom_call_target="tpu_custom_call" | custom-call | flops 6442450944 | bytes 23068672 | tf_op jit(solution)/shard_map/middle/pallas_call | solution.py:445
  79.0 2.7 slice_bitcast_fusion.4
  85.2 2.3 convolution_convert_fusion.2
  91.0 2.4 convolution_convert_fusion
  96.1 2.4 convolution_convert_fusion.1
  102.2 5.0 %collective-permute-done.11.refs_2_ = bf16[256,1024]{1,0:T(8,128)(2,1)S(1)} collective-permute-done((bf16[256,1024]{1,0:T(8,128)(2,1)S(1)}, bf16[256,1024]{1,0:T(8,128)(2,1)S(1)}, u32[]{:S(2)}, u32[]{:S(2)}) %collective-permute-start.11) | collective-permute-done | bytes 524320 | tf_op jit(solution)/shard_map/ppermute | solution.py:293
  109.5 5.6 %rows.1 = (f32[256,1024]{1,0:T(8,128)}, bf16[256,1024]{1,0:T(8,128)(2,1)}, bf16[4,256,256]{2,1,0:T(8,128)(2,1)}) custom-call(s32[1]{0:T(128)} %bitcast.where, bf16[256,1024]{1,0:T(8,128)(2,1)} %get-tuple-element.66.refs_0_, bf16[256,1024]{1,0:T(8,128)(2,1)} %copy-done.14, bf16[256,1024]{1,0:T(8,128)(2,1)} %copy-done.15, bf16[256,1024]{1,0:T(8,128)(2,1)} %copy-done.16, ...), custom_call_target="tpu_custom_call" | custom-call | flops 536870912 | bytes 8388608 | tf_op jit(solution)/shard_map/rows/pallas_call | solution.py:490
  118.1 2.0 fusion.5
  120.1 2.0 fusion.6
  124.7 6.5 %collective-permute-done.9.refs_3_ = bf16[256,1024]{1,0:T(8,128)(2,1)} collective-permute-done((bf16[256,1024]{1,0:T(8,128)(2,1)S(1)}, bf16[256,1024]{1,0:T(8,128)(2,1)}, u32[]{:S(2)}, u32[]{:S(2)}) %collective-permute-start.9) | collective-permute-done | bytes 524320 | tf_op jit(solution)/shard_map/ppermute | solution.py:293
  131.2 1.7 collective-permute-start.18
  132.9 3.8 delta.1
  138.2 1.9 pad_maximum_fusion.3.dmixed
  140.1 23.5 %back.1 = (bf16[1024,768]{1,0:T(8,128)(2,1)}, bf16[4,256,1024]{2,1,0:T(8,128)(2,1)}, f32[8,1024]{1,0:T(8,128)}) custom-call(s32[1]{0:T(128)} %bitcast.where, bf16[1024,768]{1,0:T(8,128)(2,1)} %get-tuple-element.44.qkv, bf16[1024,128]{1,0:T(8,128)(2,1)} %get-tuple-element.45.mask, bf16[4,256,256]{2,1,0:T(8,128)(2,1)} %pad_maximum_fusion.3.dmixed, ...), custom_call_target="tpu_custom_call" | custom-call | flops 2415919104 | bytes 11010048 | tf_op jit(solution)/shard_map/back/pallas_call | solution.py:523
  167.6 3.5 convolution_convert_fusion.3
  171.1 2.7 collective-permute-start.27
  173.9 2.3 collective-permute-done.27
  177.5 2.6 add_convert_fusion.2
  180.1 3.1 collective-permute-start.49
  184.8 2.3 collective-permute-start.44
  192.1 4.0 %collective-permute-done.36 = bf16[128,1024]{1,0:T(8,128)(2,1)S(1)} collective-permute-done((bf16[128,1024]{1,0:T(8,128)(2,1)S(1)}, bf16[128,1024]{1,0:T(8,128)(2,1)S(1)}, u32[]{:S(2)}, u32[]{:S(2)}) %collective-permute-start.36) | collective-permute-done | bytes 262176 | tf_op jit(solution)/shard_map/ppermute | solution.py:293
  197.4 5.0 %put_out.4.refs_0_ = bf16[8192,1024]{1,0:T(8,128)(2,1)} custom-call(s32[2]{0:T(128)} %iota_add_fusion.1.where, bf16[8192,1024]{1,0:T(8,128)(2,1)} %source.11, s32[8,128]{1,0:T(8,128)} %routes.19, bf16[256,1024]{1,0:T(8,128)(2,1)} %get-tuple-element.43.rows), custom_call_target="tpu_custom_call" | custom-call | flops 536870912 | bytes 8388608 | tf_op jit(solution)/shard_map/put_out/pallas_call | solution.py:278
  207.2 1.9 add_convert_fusion.1
  209.8 35.5 %collective-permute-done.31 = bf16[512,768]{1,0:T(8,128)(2,1)S(1)} collective-permute-done((bf16[512,768]{1,0:T(8,128)(2,1)S(1)}, bf16[512,768]{1,0:T(8,128)(2,1)S(1)}, u32[]{:S(2)}, u32[]{:S(2)}) %collective-permute-start.31) | collective-permute-done | bytes 786464 | tf_op jit(solution)/shard_map/ppermute | solution.py:313
  255.4 1.8 collective-permute-start.21
  257.6 7.2 %collective-permute-done.15.rows = bf16[256,1024]{1,0:T(8,128)(2,1)S(1)} collective-permute-done((bf16[256,1024]{1,0:T(8,128)(2,1)S(1)}, bf16[256,1024]{1,0:T(8,128)(2,1)S(1)}, u32[]{:S(2)}, u32[]{:S(2)}) %collective-permute-start.15) | collective-permute-done | bytes 524320 | tf_op jit(solution)/shard_map/ppermute | solution.py:293
  267.7 7.9 %collective-permute-done.19.refs_1_ = bf16[256,1024]{1,0:T(8,128)(2,1)S(1)} collective-permute-done((bf16[256,1024]{1,0:T(8,128)(2,1)S(1)}, bf16[256,1024]{1,0:T(8,128)(2,1)S(1)}, u32[]{:S(2)}, u32[]{:S(2)}) %collective-permute-start.19) | collective-permute-done | bytes 524320 | tf_op jit(solution)/shard_map/ppermute | solution.py:293
  278.4 5.0 %put_out.5.refs_0_ = bf16[8192,1024]{1,0:T(8,128)(2,1)} custom-call(s32[2]{0:T(128)} %iota_add_fusion.2.where, bf16[8192,1024]{1,0:T(8,128)(2,1)} %source.11, s32[8,128]{1,0:T(8,128)} %routes.19, bf16[256,1024]{1,0:T(8,128)(2,1)} %copy-done.10, bf16[8192,1024]{1,0:T(8,128)(2,1)} %put_out.4.refs_0_), custom_call_target="tpu_custom_call", output_to_operand_aliasing={{}: (4, {})} | custom-call | flops 536870912 | bytes 8388608 | tf_op jit(solution)/shard_map/put_out/pallas_call | solution.py:278
  283.9 3.0 last.1.rows
  286.9 1.8 collective-permute-start.13
  290.2 2.1 broadcast_select_fusion.2
  292.3 21.1 %collective-permute-done.51 = bf16[512,1024]{1,0:T(8,128)(2,1)} collective-permute-done((bf16[512,1024]{1,0:T(8,128)(2,1)S(1)}, bf16[512,1024]{1,0:T(8,128)(2,1)}, u32[]{:S(2)}, u32[]{:S(2)}) %collective-permute-start.51) | collective-permute-done | bytes 1048608 | tf_op jit(solution)/shard_map/ppermute | solution.py:313
  318.4 14.7 %collective-permute-done.46 = bf16[512,1024]{1,0:T(8,128)(2,1)} collective-permute-done((bf16[512,1024]{1,0:T(8,128)(2,1)S(1)}, bf16[512,1024]{1,0:T(8,128)(2,1)}, u32[]{:S(2)}, u32[]{:S(2)}) %collective-permute-start.46) | collective-permute-done | bytes 1048608 | tf_op jit(solution)/shard_map/ppermute | solution.py:313
  334.4 4.5 %collective-permute-done.41 = bf16[128,1024]{1,0:T(8,128)(2,1)S(1)} collective-permute-done((bf16[128,1024]{1,0:T(8,128)(2,1)S(1)}, bf16[128,1024]{1,0:T(8,128)(2,1)S(1)}, u32[]{:S(2)}, u32[]{:S(2)}) %collective-permute-start.41) | collective-permute-done | bytes 262176 | tf_op jit(solution)/shard_map/ppermute | solution.py:313
  340.3 5.3 %put_out.6.refs_0_ = bf16[8192,1024]{1,0:T(8,128)(2,1)} custom-call(s32[2]{0:T(128)} %iota_add_fusion.3.where, bf16[8192,1024]{1,0:T(8,128)(2,1)} %source.11, s32[8,128]{1,0:T(8,128)} %routes.19, bf16[256,1024]{1,0:T(8,128)(2,1)} %collective-permute-done.14.rows, bf16[8192,1024]{1,0:T(8,128)(2,1)} %put_out.5.refs_0_), custom_call_target="tpu_custom_call", output_to_operand_aliasing={{}: (4, {})} | custom-call | flops 536870912 | bytes 8388608 | tf_op jit(solution)/shard_map/put_out/pallas_call | solution.py:278
  345.6 5.0 %put_out.7 = bf16[8192,1024]{1,0:T(8,128)(2,1)} custom-call(s32[2]{0:T(128)} %iota_add_fusion.4.where, bf16[8192,1024]{1,0:T(8,128)(2,1)} %source.11, s32[8,128]{1,0:T(8,128)} %routes.19, bf16[256,1024]{1,0:T(8,128)(2,1)} %copy-done.11, bf16[8192,1024]{1,0:T(8,128)(2,1)} %put_out.6.refs_0_), custom_call_target="tpu_custom_call", output_to_operand_aliasing={{}: (4, {})} | custom-call | flops 536870912 | bytes 8388608 | tf_op jit(solution)/shard_map/put_out/pallas_call | solution.py:278
  350.6 5.0 %put_grad.4.refs_0_ = bf16[8192,1024]{1,0:T(8,128)(2,1)} custom-call(s32[2]{0:T(128)} %iota_add_fusion.1.where, bf16[8192,1024]{1,0:T(8,128)(2,1)} %source.15, s32[8,128]{1,0:T(8,128)} %routes.19, bf16[256,1024]{1,0:T(8,128)(2,1)} %last.1.rows), custom_call_target="tpu_custom_call" | custom-call | flops 536870912 | bytes 8388608 | tf_op jit(solution)/shard_map/put_grad/pallas_call | solution.py:278
  355.7 5.0 %put_grad.5.refs_0_ = bf16[8192,1024]{1,0:T(8,128)(2,1)} custom-call(s32[2]{0:T(128)} %iota_add_fusion.2.where, bf16[8192,1024]{1,0:T(8,128)(2,1)} %source.15, s32[8,128]{1,0:T(8,128)} %routes.19, bf16[256,1024]{1,0:T(8,128)(2,1)} %copy-done.12, bf16[8192,1024]{1,0:T(8,128)(2,1)} %put_grad.4.refs_0_), custom_call_target="tpu_custom_call", output_to_operand_aliasing={{}: (4, {})} | custom-call | flops 536870912 | bytes 8388608 | tf_op jit(solution)/shard_map/put_grad/pallas_call | solution.py:278
  360.7 5.0 %put_grad.6.refs_0_ = bf16[8192,1024]{1,0:T(8,128)(2,1)} custom-call(s32[2]{0:T(128)} %iota_add_fusion.3.where, bf16[8192,1024]{1,0:T(8,128)(2,1)} %source.15, s32[8,128]{1,0:T(8,128)} %routes.19, bf16[256,1024]{1,0:T(8,128)(2,1)} %copy-done.13, bf16[8192,1024]{1,0:T(8,128)(2,1)} %put_grad.5.refs_0_), custom_call_target="tpu_custom_call", output_to_operand_aliasing={{}: (4, {})} | custom-call | flops 536870912 | bytes 8388608 | tf_op jit(solution)/shard_map/put_grad/pallas_call | solution.py:278
  365.7 5.0 %put_grad.7 = bf16[8192,1024]{1,0:T(8,128)(2,1)} custom-call(s32[2]{0:T(128)} %iota_add_fusion.4.where, bf16[8192,1024]{1,0:T(8,128)(2,1)} %source.15, s32[8,128]{1,0:T(8,128)} %routes.19, bf16[256,1024]{1,0:T(8,128)(2,1)} %collective-permute-done.22.rows, bf16[8192,1024]{1,0:T(8,128)(2,1)} %put_grad.6.refs_0_), custom_call_target="tpu_custom_call", output_to_operand_aliasing={{}: (4, {})} | custom-call | flops 536870912 | bytes 8388608 | tf_op jit(solution)/shard_map/put_grad/pallas_call | solution.py:278
  370.8 2.1 fusion.7
  372.9 3.9 %fusion.2 = f32[1024,768]{1,0:T(8,128)} fusion(bf16[512,768]{1,0:T(8,128)(2,1)} %collective-permute-done.34, bf16[512,768]{1,0:T(8,128)(2,1)} %broadcast_select_fusion.2, pred[]{:T(512)S(6)} %eq.8), kind=kLoop, calls=%fused_computation.19 | loop fusion | flops 7864320 | bytes 4718593 | tf_op jit(solution)/shard_map/convert_element_type | solution.py:342
  376.8 4.4 %fusion.1 = f32[1024,1024]{1,0:T(8,128)} fusion(bf16[512,1024]{1,0:T(8,128)(2,1)} %collective-permute-done.52, bf16[512,1024]{1,0:T(8,128)(2,1)S(1)} %broadcast_select_fusion, pred[]{:T(512)S(6)} %eq.8), kind=kLoop, calls=%fused_computation.5 | loop fusion | flops 10485760 | bytes 6291457 | tf_op jit(solution)/shard_map/convert_element_type | solution.py:342
  381.2 2.9 fusion
  (200 shorter events, 79.3 us)
Async XLA Ops:
  1.6 33.8 %collective-permute-start.3 = (bf16[128,1024]{1,0:T(8,128)(2,1)S(1)}, bf16[128,1024]{1,0:T(8,128)(2,1)S(1)}, u32[]{:S(2)}, u32[]{:S(2)}) collective-permute-start(bf16[128,1024]{1,0:T(8,128)(2,1)S(1)} %constant_dynamic-slice_fusion.8), channel_id=1, source_target_pairs={{0,1},{1,0},{2,3},{3,2},{4,5},{5,4},{6,7},{7,6},{8,9},{9,8},{10,11... | collective-permute-start | bytes 786440 | tf_op jit(solution)/shard_map/ppermute | solution.py:293
  4.7 30.7 %collective-permute-start.4 = (bf16[128,1024]{1,0:T(8,128)(2,1)S(1)}, bf16[128,1024]{1,0:T(8,128)(2,1)S(1)}, u32[]{:S(2)}, u32[]{:S(2)}) collective-permute-start(bf16[128,1024]{1,0:T(8,128)(2,1)S(1)} %constant_dynamic-slice_fusion.8), channel_id=1, source_target_pairs={{0,2},{1,3},{2,0},{3,1},{4,6},{5,7},{6,4},{7,5},{8,10},{9,11},{10,... | collective-permute-start | bytes 786440 | tf_op jit(solution)/shard_map/ppermute | solution.py:293
  6.2 29.2 %collective-permute-start.5 = (bf16[128,1024]{1,0:T(8,128)(2,1)S(1)}, bf16[128,1024]{1,0:T(8,128)(2,1)S(1)}, u32[]{:S(2)}, u32[]{:S(2)}) collective-permute-start(bf16[128,1024]{1,0:T(8,128)(2,1)S(1)} %constant_dynamic-slice_fusion.8), channel_id=1, source_target_pairs={{0,3},{1,2},{2,1},{3,0},{4,7},{5,6},{6,5},{7,4},{8,11},{9,10},{10,... | collective-permute-start | bytes 786440 | tf_op jit(solution)/shard_map/ppermute | solution.py:293
  30.9 24.8 %collective-permute-start = (bf16[1024,256]{1,0:T(8,128)(2,1)}, bf16[1024,256]{1,0:T(8,128)(2,1)}, u32[]{:S(2)}, u32[]{:S(2)}) collective-permute-start(bf16[1024,256]{1,0:T(8,128)(2,1)} %get-tuple-element.35.refs_0_), channel_id=1, source_target_pairs={{0,1},{1,0},{2,3},{3,2},{4,5},{5,4},{6,7},{7,6},{8,9},{9,8},{10,11... | collective-permute-start | bytes 1572872 | tf_op jit(solution)/shard_map/ppermute | solution.py:293
  32.9 24.0 %collective-permute-start.1 = (bf16[1024,256]{1,0:T(8,128)(2,1)}, bf16[1024,256]{1,0:T(8,128)(2,1)S(1)}, u32[]{:S(2)}, u32[]{:S(2)}) collective-permute-start(bf16[1024,256]{1,0:T(8,128)(2,1)} %get-tuple-element.35.refs_0_), channel_id=1, source_target_pairs={{0,2},{1,3},{2,0},{3,1},{4,6},{5,7},{6,4},{7,5},{8,10},{9,11},{10,... | collective-permute-start | bytes 1572872 | tf_op jit(solution)/shard_map/ppermute | solution.py:293
  35.4 21.5 %collective-permute-start.2 = (bf16[1024,256]{1,0:T(8,128)(2,1)}, bf16[1024,256]{1,0:T(8,128)(2,1)}, u32[]{:S(2)}, u32[]{:S(2)}) collective-permute-start(bf16[1024,256]{1,0:T(8,128)(2,1)} %get-tuple-element.35.refs_0_), channel_id=1, source_target_pairs={{0,3},{1,2},{2,1},{3,0},{4,7},{5,6},{6,5},{7,4},{8,11},{9,10},{10,... | collective-permute-start | bytes 1572872 | tf_op jit(solution)/shard_map/ppermute | solution.py:293
  35.5 17.8 %collective-permute-start.6 = (bf16[3,128,1024]{2,1,0:T(8,128)(2,1)S(1)}, bf16[3,128,1024]{2,1,0:T(8,128)(2,1)S(1)}, u32[]{:S(2)}, u32[]{:S(2)}) collective-permute-start(bf16[3,128,1024]{2,1,0:T(8,128)(2,1)S(1)} %pad_maximum_fusion.2), channel_id=1, source_target_pairs={{0,4},{4,0},{8,12},{12,8},{16,20},{20,16},{24,28},{28,24},{1,5},{5... | collective-permute-start | bytes 2359304 | tf_op jit(solution)/shard_map/ppermute | solution.py:293
  81.7 19.2 %collective-permute-start.10 = (bf16[256,1024]{1,0:T(8,128)(2,1)S(1)}, bf16[256,1024]{1,0:T(8,128)(2,1)S(1)}, u32[]{:S(2)}, u32[]{:S(2)}) collective-permute-start(bf16[256,1024]{1,0:T(8,128)(2,1)S(1)} %get-tuple-element.65), channel_id=1, source_target_pairs={{0,3},{1,2},{2,1},{3,0},{4,7},{5,6},{6,5},{7,4},{8,11},{9,10},{10,... | collective-permute-start | bytes 1572872 | tf_op jit(solution)/shard_map/ppermute | solution.py:293
  83.3 23.9 %collective-permute-start.11 = (bf16[256,1024]{1,0:T(8,128)(2,1)S(1)}, bf16[256,1024]{1,0:T(8,128)(2,1)S(1)}, u32[]{:S(2)}, u32[]{:S(2)}) collective-permute-start(bf16[256,1024]{1,0:T(8,128)(2,1)S(1)} %get-tuple-element.64), channel_id=1, source_target_pairs={{0,2},{1,3},{2,0},{3,1},{4,6},{5,7},{6,4},{7,5},{8,10},{9,11},{10,... | collective-permute-start | bytes 1572872 | tf_op jit(solution)/shard_map/ppermute | solution.py:293
  83.8 24.9 %collective-permute-start.12 = (bf16[256,1024]{1,0:T(8,128)(2,1)S(1)}, bf16[256,1024]{1,0:T(8,128)(2,1)S(1)}, u32[]{:S(2)}, u32[]{:S(2)}) collective-permute-start(bf16[256,1024]{1,0:T(8,128)(2,1)S(1)} %get-tuple-element.63), channel_id=1, source_target_pairs={{0,1},{1,0},{2,3},{3,2},{4,5},{5,4},{6,7},{7,6},{8,9},{9,8},{10,11... | collective-permute-start | bytes 1572872 | tf_op jit(solution)/shard_map/ppermute | solution.py:293
  88.7 34.1 %collective-permute-start.7 = (bf16[256,1024]{1,0:T(8,128)(2,1)}, bf16[256,1024]{1,0:T(8,128)(2,1)}, u32[]{:S(2)}, u32[]{:S(2)}) collective-permute-start(bf16[256,1024]{1,0:T(8,128)(2,1)} %get-tuple-element.69), channel_id=1, source_target_pairs={{0,1},{1,0},{2,3},{3,2},{4,5},{5,4},{6,7},{7,6},{8,9},{9,8},{10,11... | collective-permute-start | bytes 1572872 | tf_op jit(solution)/shard_map/ppermute | solution.py:293
  89.4 34.1 %collective-permute-start.8 = (bf16[256,1024]{1,0:T(8,128)(2,1)}, bf16[256,1024]{1,0:T(8,128)(2,1)}, u32[]{:S(2)}, u32[]{:S(2)}) collective-permute-start(bf16[256,1024]{1,0:T(8,128)(2,1)} %get-tuple-element.68), channel_id=1, source_target_pairs={{0,2},{1,3},{2,0},{3,1},{4,6},{5,7},{6,4},{7,5},{8,10},{9,11},{10,... | collective-permute-start | bytes 1572872 | tf_op jit(solution)/shard_map/ppermute | solution.py:293
  100.9 30.3 %collective-permute-start.9 = (bf16[256,1024]{1,0:T(8,128)(2,1)S(1)}, bf16[256,1024]{1,0:T(8,128)(2,1)}, u32[]{:S(2)}, u32[]{:S(2)}) collective-permute-start(bf16[256,1024]{1,0:T(8,128)(2,1)S(1)} %get-tuple-element.67), channel_id=1, source_target_pairs={{0,3},{1,2},{2,1},{3,0},{4,7},{5,6},{6,5},{7,4},{8,11},{9,10},{10,... | collective-permute-start | bytes 1572872 | tf_op jit(solution)/shard_map/ppermute | solution.py:293
  107.2 70.3 %collective-permute-start.48 = (bf16[512,1024]{1,0:T(8,128)(2,1)}, bf16[512,1024]{1,0:T(8,128)(2,1)}, u32[]{:S(2)}, u32[]{:S(2)}) collective-permute-start(bf16[512,1024]{1,0:T(8,128)(2,1)} %constant_dynamic-slice_fusion), channel_id=1, source_target_pairs={{0,4},{4,0},{8,12},{12,8},{16,20},{20,16},{24,28},{28,24},{1,5},{5... | collective-permute-start | bytes 3145736 | tf_op jit(solution)/shard_map/ppermute | solution.py:293
  108.7 74.5 %collective-permute-start.43 = (bf16[512,1024]{1,0:T(8,128)(2,1)}, bf16[512,1024]{1,0:T(8,128)(2,1)}, u32[]{:S(2)}, u32[]{:S(2)}) collective-permute-start(bf16[512,1024]{1,0:T(8,128)(2,1)} %constant_dynamic-slice_fusion.1), channel_id=1, source_target_pairs={{0,4},{4,0},{8,12},{12,8},{16,20},{20,16},{24,28},{28,24},{1,5},{5... | collective-permute-start | bytes 3145736 | tf_op jit(solution)/shard_map/ppermute | solution.py:293
  122.8 15.4 %collective-permute-start.16 = (bf16[256,256]{1,0:T(8,128)(2,1)}, bf16[256,256]{1,0:T(8,128)(2,1)}, u32[]{:S(2)}, u32[]{:S(2)}) collective-permute-start(bf16[256,256]{1,0:T(8,128)(2,1)} %get-tuple-element.77), channel_id=1, source_target_pairs={{0,1},{1,0},{2,3},{3,2},{4,5},{5,4},{6,7},{7,6},{8,9},{9,8},{10,11... | collective-permute-start | bytes 393224 | tf_op jit(solution)/shard_map/ppermute | solution.py:293
  123.5 14.7 %collective-permute-start.17 = (bf16[256,256]{1,0:T(8,128)(2,1)S(1)}, bf16[256,256]{1,0:T(8,128)(2,1)}, u32[]{:S(2)}, u32[]{:S(2)}) collective-permute-start(bf16[256,256]{1,0:T(8,128)(2,1)S(1)} %get-tuple-element.76), channel_id=1, source_target_pairs={{0,2},{1,3},{2,0},{3,1},{4,6},{5,7},{6,4},{7,5},{8,10},{9,11},{10,... | collective-permute-start | bytes 393224 | tf_op jit(solution)/shard_map/ppermute | solution.py:293
  164.8 22.3 %collective-permute-start.35 = (bf16[128,4,1024]{2,0,1:T(8,128)(2,1)S(1)}, bf16[128,4,1024]{2,0,1:T(8,128)(2,1)S(1)}, u32[]{:S(2)}, u32[]{:S(2)}) collective-permute-start(bf16[128,4,1024]{2,0,1:T(8,128)(2,1)S(1)} %constant_dynamic-slice_fusion.2), channel_id=1, source_target_pairs={{0,4},{4,0},{8,12},{12,8},{16,20},{20,16},{24,28},{28,24},{1,5},{5... | collective-permute-start | bytes 3145736 | tf_op jit(solution)/shard_map/ppermute | solution.py:293
  173.8 16.2 %collective-permute-start.30 = (bf16[512,768]{1,0:T(8,128)(2,1)S(1)}, bf16[512,768]{1,0:T(8,128)(2,1)S(1)}, u32[]{:S(2)}, u32[]{:S(2)}) collective-permute-start(bf16[512,768]{1,0:T(8,128)(2,1)S(1)} %constant_dynamic-slice_fusion.3), channel_id=1, source_target_pairs={{0,4},{4,0},{8,12},{12,8},{16,20},{20,16},{24,28},{28,24},{1,5},{5... | collective-permute-start | bytes 2359304 | tf_op jit(solution)/shard_map/ppermute | solution.py:293
  176.2 15.3 %collective-permute-start.28 = (f32[8,1024]{1,0:T(8,128)S(1)}, f32[8,1024]{1,0:T(8,128)S(1)}, u32[]{:S(2)}, u32[]{:S(2)}) collective-permute-start(f32[8,1024]{1,0:T(8,128)S(1)} %add.167), channel_id=1, source_target_pairs={{0,1},{1,0},{2,3},{3,2},{4,5},{5,4},{6,7},{7,6},{8,9},{9,8},{10,11... | collective-permute-start | bytes 98312 | tf_op jit(solution)/shard_map/ppermute | solution.py:293
  180.1 27.1 %collective-permute-start.49 = (bf16[512,1024]{1,0:T(8,128)(2,1)}, bf16[512,1024]{1,0:T(8,128)(2,1)}, u32[]{:S(2)}, u32[]{:S(2)}) collective-permute-start(bf16[512,1024]{1,0:T(8,128)(2,1)} %add_convert_fusion.2), channel_id=1, source_target_pairs={{0,8},{4,12},{24,16},{28,20},{1,9},{5,13},{25,17},{29,21},{2,10},{... | collective-permute-start | bytes 3145736 | tf_op jit(solution)/shard_map/ppermute | solution.py:313
  184.8 61.5 %collective-permute-start.44 = (bf16[512,1024]{1,0:T(8,128)(2,1)S(1)}, bf16[512,1024]{1,0:T(8,128)(2,1)}, u32[]{:S(2)}, u32[]{:S(2)}) collective-permute-start(bf16[512,1024]{1,0:T(8,128)(2,1)S(1)} %add_convert_fusion.5), channel_id=1, source_target_pairs={{0,8},{4,12},{24,16},{28,20},{1,9},{5,13},{25,17},{29,21},{2,10},{... | collective-permute-start | bytes 3145736 | tf_op jit(solution)/shard_map/ppermute | solution.py:313
  190.1 55.2 %collective-permute-start.31 = (bf16[512,768]{1,0:T(8,128)(2,1)S(1)}, bf16[512,768]{1,0:T(8,128)(2,1)S(1)}, u32[]{:S(2)}, u32[]{:S(2)}) collective-permute-start(bf16[512,768]{1,0:T(8,128)(2,1)S(1)} %add_convert_fusion.9), channel_id=1, source_target_pairs={{0,8},{4,12},{24,16},{28,20},{1,9},{5,13},{25,17},{29,21},{2,10},{... | collective-permute-start | bytes 2359304 | tf_op jit(solution)/shard_map/ppermute | solution.py:313
  191.5 12.6 %collective-permute-start.37 = (bf16[128,1024]{1,0:T(8,128)(2,1)}, bf16[128,1024]{1,0:T(8,128)(2,1)S(1)}, u32[]{:S(2)}, u32[]{:S(2)}) collective-permute-start(bf16[128,1024]{1,0:T(8,128)(2,1)} %get-tuple-element.73), channel_id=1, source_target_pairs={{0,2},{1,3},{2,0},{3,1},{4,6},{5,7},{6,4},{7,5},{8,10},{9,11},{10,... | collective-permute-start | bytes 786440 | tf_op jit(solution)/shard_map/ppermute | solution.py:293
  196.1 8.5 %collective-permute-start.38 = (bf16[128,1024]{1,0:T(8,128)(2,1)S(1)}, bf16[128,1024]{1,0:T(8,128)(2,1)}, u32[]{:S(2)}, u32[]{:S(2)}) collective-permute-start(bf16[128,1024]{1,0:T(8,128)(2,1)S(1)} %get-tuple-element.72), channel_id=1, source_target_pairs={{0,3},{1,2},{2,1},{3,0},{4,7},{5,6},{6,5},{7,4},{8,11},{9,10},{10,... | collective-permute-start | bytes 786440 | tf_op jit(solution)/shard_map/ppermute | solution.py:293
  204.1 45.9 %collective-permute-start.29 = (f32[8,1024]{1,0:T(8,128)S(1)}, f32[8,1024]{1,0:T(8,128)S(1)}, u32[]{:S(2)}, u32[]{:S(2)}) collective-permute-start(f32[8,1024]{1,0:T(8,128)S(1)} %add.168), channel_id=1, source_target_pairs={{0,2},{1,3},{2,0},{3,1},{4,6},{5,7},{6,4},{7,5},{8,10},{9,11},{10,... | collective-permute-start | bytes 98312 | tf_op jit(solution)/shard_map/ppermute | solution.py:293
  205.8 47.3 %collective-permute-start.39 = (bf16[128,1024]{1,0:T(8,128)(2,1)S(1)}, bf16[128,1024]{1,0:T(8,128)(2,1)S(1)}, u32[]{:S(2)}, u32[]{:S(2)}) collective-permute-start(bf16[128,1024]{1,0:T(8,128)(2,1)S(1)} %fusion.10), channel_id=1, source_target_pairs={{0,8},{4,12},{24,16},{28,20},{1,9},{5,13},{25,17},{29,21},{2,10},{... | collective-permute-start | bytes 786440 | tf_op jit(solution)/shard_map/ppermute | solution.py:313
  209.1 46.3 %collective-permute-start.50 = (bf16[512,1024]{1,0:T(8,128)(2,1)S(1)}, bf16[512,1024]{1,0:T(8,128)(2,1)S(1)}, u32[]{:S(2)}, u32[]{:S(2)}) collective-permute-start(bf16[512,1024]{1,0:T(8,128)(2,1)S(1)} %add_convert_fusion.1), channel_id=1, source_target_pairs={{8,16},{12,20},{16,8},{20,12},{9,17},{13,21},{17,9},{21,13},{10,18... | collective-permute-start | bytes 3145736 | tf_op jit(solution)/shard_map/ppermute | solution.py:313
  245.5 9.1 %collective-permute-start.32 = (bf16[512,768]{1,0:T(8,128)(2,1)S(1)}, bf16[512,768]{1,0:T(8,128)(2,1)S(1)}, u32[]{:S(2)}, u32[]{:S(2)}) collective-permute-start(bf16[512,768]{1,0:T(8,128)(2,1)S(1)} %add_convert_fusion.8), channel_id=1, source_target_pairs={{8,16},{12,20},{16,8},{20,12},{9,17},{13,21},{17,9},{21,13},{10,18... | collective-permute-start | bytes 2359304 | tf_op jit(solution)/shard_map/ppermute | solution.py:313
  248.0 18.0 %collective-permute-start.45 = (bf16[512,1024]{1,0:T(8,128)(2,1)S(1)}, bf16[512,1024]{1,0:T(8,128)(2,1)S(1)}, u32[]{:S(2)}, u32[]{:S(2)}) collective-permute-start(bf16[512,1024]{1,0:T(8,128)(2,1)S(1)} %add_convert_fusion.4), channel_id=1, source_target_pairs={{8,16},{12,20},{16,8},{20,12},{9,17},{13,21},{17,9},{21,13},{10,18... | collective-permute-start | bytes 3145736 | tf_op jit(solution)/shard_map/ppermute | solution.py:313
  249.9 14.8 %collective-permute-start.15 = (bf16[256,1024]{1,0:T(8,128)(2,1)S(1)}, bf16[256,1024]{1,0:T(8,128)(2,1)S(1)}, u32[]{:S(2)}, u32[]{:S(2)}) collective-permute-start(bf16[256,1024]{1,0:T(8,128)(2,1)S(1)} %copy-done.9), channel_id=1, source_target_pairs={{0,1},{1,0},{2,3},{3,2},{4,5},{5,4},{6,7},{7,6},{8,9},{9,8},{10,11... | collective-permute-start | bytes 1572872 | tf_op jit(solution)/shard_map/ppermute | solution.py:293
  253.2 22.5 %collective-permute-start.19 = (bf16[256,1024]{1,0:T(8,128)(2,1)S(1)}, bf16[256,1024]{1,0:T(8,128)(2,1)S(1)}, u32[]{:S(2)}, u32[]{:S(2)}) collective-permute-start(bf16[256,1024]{1,0:T(8,128)(2,1)S(1)} %get-tuple-element.61), channel_id=1, source_target_pairs={{0,1},{1,0},{2,3},{3,2},{4,5},{5,4},{6,7},{7,6},{8,9},{9,8},{10,11... | collective-permute-start | bytes 1572872 | tf_op jit(solution)/shard_map/ppermute | solution.py:293
  254.6 21.8 %collective-permute-start.20 = (bf16[256,1024]{1,0:T(8,128)(2,1)S(1)}, bf16[256,1024]{1,0:T(8,128)(2,1)S(1)}, u32[]{:S(2)}, u32[]{:S(2)}) collective-permute-start(bf16[256,1024]{1,0:T(8,128)(2,1)S(1)} %get-tuple-element.60), channel_id=1, source_target_pairs={{0,2},{1,3},{2,0},{3,1},{4,6},{5,7},{6,4},{7,5},{8,10},{9,11},{10,... | collective-permute-start | bytes 1572872 | tf_op jit(solution)/shard_map/ppermute | solution.py:293
  255.4 28.0 %collective-permute-start.21 = (bf16[256,1024]{1,0:T(8,128)(2,1)}, bf16[256,1024]{1,0:T(8,128)(2,1)}, u32[]{:S(2)}, u32[]{:S(2)}) collective-permute-start(bf16[256,1024]{1,0:T(8,128)(2,1)} %get-tuple-element.59), channel_id=1, source_target_pairs={{0,3},{1,2},{2,1},{3,0},{4,7},{5,6},{6,5},{7,4},{8,11},{9,10},{10,... | collective-permute-start | bytes 1572872 | tf_op jit(solution)/shard_map/ppermute | solution.py:293
  264.7 24.1 %collective-permute-start.33 = (bf16[512,768]{1,0:T(8,128)(2,1)S(1)}, bf16[512,768]{1,0:T(8,128)(2,1)}, u32[]{:S(2)}, u32[]{:S(2)}) collective-permute-start(bf16[512,768]{1,0:T(8,128)(2,1)S(1)} %add_convert_fusion.7), channel_id=1, source_target_pairs={{8,0},{12,4},{16,24},{20,28},{9,1},{13,5},{17,25},{21,29},{10,2},{... | collective-permute-start | bytes 2359304 | tf_op jit(solution)/shard_map/ppermute | solution.py:313
  266.0 47.4 %collective-permute-start.51 = (bf16[512,1024]{1,0:T(8,128)(2,1)S(1)}, bf16[512,1024]{1,0:T(8,128)(2,1)}, u32[]{:S(2)}, u32[]{:S(2)}) collective-permute-start(bf16[512,1024]{1,0:T(8,128)(2,1)S(1)} %add_convert_fusion), channel_id=1, source_target_pairs={{8,0},{12,4},{16,24},{20,28},{9,1},{13,5},{17,25},{21,29},{10,2},{... | collective-permute-start | bytes 3145736 | tf_op jit(solution)/shard_map/ppermute | solution.py:313
  275.7 11.2 %collective-permute-start.40 = (bf16[128,1024]{1,0:T(8,128)(2,1)S(1)}, bf16[128,1024]{1,0:T(8,128)(2,1)S(1)}, u32[]{:S(2)}, u32[]{:S(2)}) collective-permute-start(bf16[128,1024]{1,0:T(8,128)(2,1)S(1)} %add_convert_fusion.11), channel_id=1, source_target_pairs={{8,16},{12,20},{16,8},{20,12},{9,17},{13,21},{17,9},{21,13},{10,18... | collective-permute-start | bytes 786440 | tf_op jit(solution)/shard_map/ppermute | solution.py:313
  276.5 56.6 %collective-permute-start.46 = (bf16[512,1024]{1,0:T(8,128)(2,1)S(1)}, bf16[512,1024]{1,0:T(8,128)(2,1)}, u32[]{:S(2)}, u32[]{:S(2)}) collective-permute-start(bf16[512,1024]{1,0:T(8,128)(2,1)S(1)} %add_convert_fusion.3), channel_id=1, source_target_pairs={{8,0},{12,4},{16,24},{20,28},{9,1},{13,5},{17,25},{21,29},{10,2},{... | collective-permute-start | bytes 3145736 | tf_op jit(solution)/shard_map/ppermute | solution.py:313
  283.4 31.8 %collective-permute-start.14 = (bf16[256,1024]{1,0:T(8,128)(2,1)}, bf16[256,1024]{1,0:T(8,128)(2,1)}, u32[]{:S(2)}, u32[]{:S(2)}) collective-permute-start(bf16[256,1024]{1,0:T(8,128)(2,1)} %get-tuple-element.43.rows), channel_id=1, source_target_pairs={{0,2},{1,3},{2,0},{3,1},{4,6},{5,7},{6,4},{7,5},{8,10},{9,11},{10,... | collective-permute-start | bytes 1572872 | tf_op jit(solution)/shard_map/ppermute | solution.py:293
  286.9 30.1 %collective-permute-start.13 = (bf16[256,1024]{1,0:T(8,128)(2,1)}, bf16[256,1024]{1,0:T(8,128)(2,1)S(1)}, u32[]{:S(2)}, u32[]{:S(2)}) collective-permute-start(bf16[256,1024]{1,0:T(8,128)(2,1)} %get-tuple-element.43.rows), channel_id=1, source_target_pairs={{0,3},{1,2},{2,1},{3,0},{4,7},{5,6},{6,5},{7,4},{8,11},{9,10},{10,... | collective-permute-start | bytes 1572872 | tf_op jit(solution)/shard_map/ppermute | solution.py:293
  288.8 29.5 %collective-permute-start.24 = (bf16[256,1024]{1,0:T(8,128)(2,1)}, bf16[256,1024]{1,0:T(8,128)(2,1)S(1)}, u32[]{:S(2)}, u32[]{:S(2)}) collective-permute-start(bf16[256,1024]{1,0:T(8,128)(2,1)} %last.1.rows), channel_id=1, source_target_pairs={{0,1},{1,0},{2,3},{3,2},{4,5},{5,4},{6,7},{7,6},{8,9},{9,8},{10,11... | collective-permute-start | bytes 1572872 | tf_op jit(solution)/shard_map/ppermute | solution.py:293
  313.4 25.6 %collective-permute-start.23 = (bf16[256,1024]{1,0:T(8,128)(2,1)}, bf16[256,1024]{1,0:T(8,128)(2,1)S(1)}, u32[]{:S(2)}, u32[]{:S(2)}) collective-permute-start(bf16[256,1024]{1,0:T(8,128)(2,1)} %last.1.rows), channel_id=1, source_target_pairs={{0,2},{1,3},{2,0},{3,1},{4,6},{5,7},{6,4},{7,5},{8,10},{9,11},{10,... | collective-permute-start | bytes 1572872 | tf_op jit(solution)/shard_map/ppermute | solution.py:293
  315.3 50.5 %collective-permute-start.22 = (bf16[256,1024]{1,0:T(8,128)(2,1)}, bf16[256,1024]{1,0:T(8,128)(2,1)}, u32[]{:S(2)}, u32[]{:S(2)}) collective-permute-start(bf16[256,1024]{1,0:T(8,128)(2,1)} %last.1.rows), channel_id=1, source_target_pairs={{0,3},{1,2},{2,1},{3,0},{4,7},{5,6},{6,5},{7,4},{8,11},{9,10},{10,... | collective-permute-start | bytes 1572872 | tf_op jit(solution)/shard_map/ppermute | solution.py:293
  317.0 21.9 %collective-permute-start.41 = (bf16[128,1024]{1,0:T(8,128)(2,1)S(1)}, bf16[128,1024]{1,0:T(8,128)(2,1)S(1)}, u32[]{:S(2)}, u32[]{:S(2)}) collective-permute-start(bf16[128,1024]{1,0:T(8,128)(2,1)S(1)} %add_convert_fusion.10), channel_id=1, source_target_pairs={{8,0},{12,4},{16,24},{20,28},{9,1},{13,5},{17,25},{21,29},{10,2},{... | collective-permute-start | bytes 786440 | tf_op jit(solution)/shard_map/ppermute | solution.py:313
  318.3 54.6 %collective-permute-start.34 = (bf16[512,768]{1,0:T(8,128)(2,1)}, bf16[512,768]{1,0:T(8,128)(2,1)}, u32[]{:S(2)}, u32[]{:S(2)}) collective-permute-start(bf16[512,768]{1,0:T(8,128)(2,1)} %broadcast_select_fusion.2), channel_id=1, source_target_pairs={{0,4},{4,0},{8,12},{12,8},{16,20},{20,16},{24,28},{28,24},{1,5},{5... | collective-permute-start | bytes 2359304 | tf_op jit(solution)/shard_map/ppermute | solution.py:293
  333.1 43.7 %collective-permute-start.52 = (bf16[512,1024]{1,0:T(8,128)(2,1)S(1)}, bf16[512,1024]{1,0:T(8,128)(2,1)}, u32[]{:S(2)}, u32[]{:S(2)}) collective-permute-start(bf16[512,1024]{1,0:T(8,128)(2,1)S(1)} %broadcast_select_fusion), channel_id=1, source_target_pairs={{0,4},{4,0},{8,12},{12,8},{16,20},{20,16},{24,28},{28,24},{1,5},{5... | collective-permute-start | bytes 3145736 | tf_op jit(solution)/shard_map/ppermute | solution.py:293
  338.9 42.2 %collective-permute-start.47 = (bf16[512,1024]{1,0:T(8,128)(2,1)S(1)}, bf16[512,1024]{1,0:T(8,128)(2,1)S(1)}, u32[]{:S(2)}, u32[]{:S(2)}) collective-permute-start(bf16[512,1024]{1,0:T(8,128)(2,1)S(1)} %broadcast_select_fusion.1), channel_id=1, source_target_pairs={{0,4},{4,0},{8,12},{12,8},{16,20},{20,16},{24,28},{28,24},{1,5},{5... | collective-permute-start | bytes 3145736 | tf_op jit(solution)/shard_map/ppermute | solution.py:293
  339.8 31.0 %collective-permute-start.42 = (bf16[128,1024]{1,0:T(8,128)(2,1)S(1)}, bf16[128,1024]{1,0:T(8,128)(2,1)}, u32[]{:S(2)}, u32[]{:S(2)}) collective-permute-start(bf16[128,1024]{1,0:T(8,128)(2,1)S(1)} %broadcast_select_fusion.3), channel_id=1, source_target_pairs={{0,4},{4,0},{8,12},{12,8},{16,20},{20,16},{24,28},{28,24},{1,5},{5... | collective-permute-start | bytes 786440 | tf_op jit(solution)/shard_map/ppermute | solution.py:293
  (34 other events, 226.6 us)
